TPU v7x, 512 devices: a whole 4x4x16 slice. The times are simulated.
512 devices in a mesh: grp: 16 (over z_lo, y), band: 32 (over z_hi, x, core).
Axes of the slice: x: 4, y: 4, z: 16 (z_hi: 4, z_lo: 4; z = z_hi * 4 + z_lo), core: 2. Of those that a mesh axis runs over, the one named last changes fastest.
Arguments:
- raw: bfloat16 [2, 256, 262144], P(None, 'band', 'grp'), may hold values from -6 to 6
- taps: int32 [5, 2, 4, 512], replicated, may hold values from 0 to 255, as said below
- weights: float32 [5, 2, 4, 512], replicated, may hold values from -0.11 to 1.6, as said below
- shifts: float32 [5], replicated, may hold values from 1 to 3
Outputs:
- image: bfloat16 [2, 262144, 256], P(None, ('grp', 'band'))
Inputs may be any that keep to these rules, and one draw needn't show every extreme that they name: taps[l, h, s, j] = c - 1 + s clipped to the half sector, where c is j / 2 or (j + 1) / 2 rounded down, clipped likewise. `weights`: each group of four coefficients is a cubic Lagrange stencil times a positive factor.
All inputs are finite; a program needn't handle non-finite values.
Results may differ from a plain program's by a relative error of at most 0.011.
Values may be sent and summed in bfloat16 or wider, within the bound.
A program may use at most 64 MiB of HBM per device.

v0:
```python
import math

import jax
import jax.numpy as jnp
from jax import lax
from jax.sharding import Mesh
from jax.sharding import PartitionSpec as P

ANGLES = 512
BAND_LEVELS = 3
LEVELS = 5
BAND = ("band_0", "band_1", "band_2")
GRP_BAND = ("grp", "band_0", "band_1", "band_2")


inv_root_two = 0.7071067811865476


def swapped(block, axis, apart):
    count = lax.axis_size(axis)
    route = []
    for low in range(count):
        high = low | 1 << apart
        if high != low and high < count:
            route += [(low, high), (high, low)]
    return lax.ppermute(block, axis, route)


def cut_along(value, dim, length):
    lengths = value.shape
    parts = value.reshape(*lengths[:dim], length, lengths[dim] // length, *lengths[dim + 1 :])
    return jnp.moveaxis(parts, dim, 0)


def in_order(parts, dim):
    lengths = list(parts.shape[1:])
    lengths[dim] *= parts.shape[0]
    return jnp.moveaxis(parts, 0, dim).reshape(lengths)


def moved_by_axis(parts, axes, sequence):
    lengths = [lax.axis_size(a) for a in axes]
    parts = parts.reshape(*lengths, *parts.shape[1:])
    for k in sequence:
        parts = lax.all_to_all(parts, axes[k], split_axis=k, concat_axis=k, tiled=True)
    return parts.reshape(-1, *parts.shape[len(axes) :])


def exchange_by_chip(value, groups, sequence, split_dim, concat_dim):
    length = lax.axis_size(groups[0]) * lax.axis_size(groups[1])
    parts = cut_along(value, split_dim, length)
    return in_order(moved_by_axis(parts, groups, sequence), concat_dim)


def range_table(freq_count):
    column = jnp.arange(freq_count, dtype=jnp.int32)
    phases = (column[:, None] * column[None, :] % freq_count).astype(jnp.float32) * (
        2.0 * math.pi / freq_count
    )
    cosine = jnp.cos(phases)
    sine_map = jnp.sin(phases)
    real_rows = jnp.stack([cosine, -sine_map], axis=1)
    imag_rows = jnp.stack([sine_map, cosine], axis=1)
    return jnp.stack([real_rows, imag_rows], axis=0).astype(jnp.bfloat16)


def beam_table(angles, pulses):
    angle_ids = jnp.arange(angles, dtype=jnp.int32)
    pulse_ids = jnp.arange(pulses, dtype=jnp.int32)
    phases = (angle_ids[:, None] * pulse_ids[None, :] % angles).astype(jnp.float32) * (
        2.0 * math.pi / angles
    )
    cosine = jnp.cos(phases)
    sine_map = jnp.sin(phases)
    real_rows = jnp.stack([cosine, sine_map], axis=1)
    imag_rows = jnp.stack([-sine_map, cosine], axis=1)
    return jnp.stack([real_rows, imag_rows], axis=0).astype(jnp.bfloat16)


def interp_matrix(tap_rows, weight_rows, half_len):
    onehot = tap_rows[:, :, None] == jnp.arange(half_len, dtype=jnp.int32)[None, None, :]
    matrix = jnp.sum(
        jnp.where(onehot, weight_rows[:, :, None], jnp.zeros((), weight_rows.dtype)), axis=0
    )
    return matrix.astype(jnp.bfloat16)


def phase_angle(shift_now, half_bit, angles, freq_count):
    angle_pos = (half_bit * angles + jnp.arange(angles, dtype=jnp.int32)).astype(jnp.float32)
    across = (angle_pos + 0.5) / (2.0 * angles) - 0.5
    ranges = (jnp.arange(freq_count, dtype=jnp.int32) + freq_count).astype(jnp.float32) / freq_count
    return 2.0 * math.pi * shift_now * across[:, None] * ranges[None, :]


def rotate(real_part, imag_part, cosine, sine_map):
    return (cosine * real_part - sine_map * imag_part, cosine * imag_part + sine_map * real_part)


def swap_half(piece_half, section_no):
    if section_no == 0:
        return swapped(piece_half, BAND, 0)
    if section_no < BAND_LEVELS:
        return swapped(piece_half, BAND, section_no)
    return swapped(piece_half, "grp", section_no - BAND_LEVELS)


def merge_level(section_no, half_bit, own_half, fetch_half, taps, weights, shifts):
    half_len = own_half.shape[1]
    angles = 2 * half_len
    freq_count = own_half.shape[2]
    tap_rows = lax.dynamic_index_in_dim(taps[section_no], half_bit, 0, keepdims=False)
    weight_rows = lax.dynamic_index_in_dim(weights[section_no], half_bit, 0, keepdims=False)
    matrix = interp_matrix(tap_rows, weight_rows, half_len)
    angle_map = phase_angle(shifts[section_no], half_bit, angles, freq_count)
    cosine = jnp.cos(angle_map)
    sine_map = jnp.sin(angle_map)
    own_sign = (1 - 2 * half_bit).astype(jnp.float32)
    partner = fetch_half()
    stacked = jnp.einsum(
        "jk,ncks->ncjs", matrix, jnp.stack([own_half, partner]), preferred_element_type=jnp.float32
    )
    own_prod = stacked[0]
    partner_prod = stacked[1]
    own_sine = own_sign * sine_map
    own_re, own_im = rotate(own_prod[0], own_prod[1], cosine, own_sine)
    partner_re, partner_im = rotate(partner_prod[0], partner_prod[1], cosine, -own_sine)
    merged = jnp.stack([own_re + partner_re, own_im + partner_im]) * inv_root_two
    return merged.astype(jnp.bfloat16)


def later_fetch(sent_half, section_no):

    def fetch_half():
        return swap_half(sent_half, section_no)

    return fetch_half


def on_device(raw, taps, weights, shifts):
    samples = exchange_by_chip(raw, (("band_0", "band_1"), "band_2"), (1, 0), 2, 1)
    freq_count = samples.shape[1]
    pulses = samples.shape[2]
    half_len = ANGLES // 2
    profile = (
        jnp.einsum(
            "cfq,cfds->dqs", samples, range_table(freq_count), preferred_element_type=jnp.float32
        )
        * (1.0 / math.sqrt(freq_count))
    ).astype(jnp.bfloat16)
    beam_full = beam_table(ANGLES, pulses)
    band_pos = lax.axis_index(BAND)
    grp_pos = lax.axis_index("grp")

    def bit_of(section_no):
        if section_no < BAND_LEVELS:
            return band_pos >> section_no & 1
        return grp_pos >> section_no - BAND_LEVELS & 1

    half_bit = bit_of(0)
    product = jnp.einsum("dacq,cqr->dar", beam_full, profile, preferred_element_type=jnp.float32)
    whole = (product * (1.0 / math.sqrt(pulses))).astype(jnp.bfloat16)
    kept_half = lax.dynamic_slice_in_dim(whole, half_bit * half_len, half_len, 1)
    sent_half = lax.dynamic_slice_in_dim(whole, (1 - half_bit) * half_len, half_len, 1)
    images = merge_level(
        0, half_bit, kept_half, lambda: swap_half(sent_half, 0), taps, weights, shifts
    )
    for section_no in range(1, LEVELS):
        level_bit = bit_of(section_no)
        kept_half = lax.dynamic_slice_in_dim(images, level_bit * half_len, half_len, 1)
        sent_half = lax.dynamic_slice_in_dim(images, (1 - level_bit) * half_len, half_len, 1)
        images = merge_level(
            section_no,
            level_bit,
            kept_half,
            later_fetch(sent_half, section_no),
            taps,
            weights,
            shifts,
        )
    return images


def solution(mesh):
    split = Mesh(
        mesh.devices.reshape(mesh.shape["grp"], 4, 4, 2), ("grp", "band_0", "band_1", "band_2")
    )
    return jax.shard_map(
        on_device,
        mesh=split,
        in_specs=(P(None, BAND, "grp"), P(), P(), P()),
        out_specs=P(None, GRP_BAND, None),
        check_vma=False,
    )
```

profile of v0, /device:TPU:40, one launch (start us, length us, event | category | flops | bytes accessed | tf_op | source)
XLA Modules:
  0.0 118.2 jit_solution(16325214566109520538)
XLA Ops:
  0.0 1.2 %copy.53 = bf16[2,8,32,512]{3,2,1,0:T(8,128)(2,1)S(1)} copy(bf16[2,8,32,512]{3,1,2,0:T(8,128)(2,1)} %bitcast.250) | data formatting | bytes 1048576
  1.2 0.3 copy.28
  1.5 0.0 copy-start
  1.5 0.0 copy-start.1
  1.5 0.0 copy-start.2
  1.6 4.3 %all_to_all.10 = bf16[16,2,2,8,512]{4,3,0,2,1:T(8,128)(2,1)S(1)} all-to-all(bf16[16,2,2,8,512]{4,3,0,2,1:T(8,128)(2,1)S(1)} %copy.29), channel_id=1, replica_groups=mesh['grp'=16,'band_0'=4,'band_1'=4,'band_2'=2] {'band_2'}, dimensions={1} | all-to-all | bytes 1048576 | tf_op jit(solution)/shard_map/all_to_all | solution.py:45
  5.9 0.9 copy.30
  6.7 16.8 %all-to-all-start.1 = ((bf16[16,2,2,8,512]{4,3,1,2,0:T(8,128)(2,1)}), bf16[16,2,2,8,512]{4,3,1,2,0:T(8,128)(2,1)S(1)}, u32[]{:S(2)}, u32[]{:S(2)}) async-start(bf16[16,2,2,8,512]{4,3,1,2,0:T(8,128)(2,1)} %copy.30), calls=%async_computation.1 | async-start | bytes 1048576 | tf_op jit(solution)/shard_map/all_to_all | solution.py:45
  23.5 0.0 copy-done
  23.5 0.0 copy-done.1
  23.5 0.0 copy-done.2
  23.6 0.7 fusion.163
  27.5 1.0 fusion.152
  28.5 1.1 negate_convert_fusion.1
  29.6 4.0 %fusion.134 = bf16[512,1,512]{2,0,1:T(8,128)(2,1)S(1)} fusion(), kind=kLoop, calls=%fused_computation.182 | loop fusion | flops 3932160 | bytes 524288 | tf_op jit(solution)/shard_map/convert.15
  33.6 0.7 maximum_bitcast_fusion.2
  34.3 4.3 %negate_convert_fusion = (bf16[512,1,512]{2,0,1:T(8,128)(2,1)S(1)}, bf16[512,1,512]{2,0,1:T(8,128)(2,1)S(1)}) fusion(), kind=kLoop, calls=%fused_computation.44 | loop fusion | flops 4456448 | bytes 1048576 | tf_op jit(solution)/shard_map/convert.11
  38.7 0.2 maximum_bitcast_fusion
  38.9 16.3 %all-to-all-done.1 = bf16[16,2,2,8,512]{4,3,1,2,0:T(8,128)(2,1)S(1)} async-done(((bf16[16,2,2,8,512]{4,3,1,2,0:T(8,128)(2,1)}), bf16[16,2,2,8,512]{4,3,1,2,0:T(8,128)(2,1)S(1)}, u32[]{:S(2)}, u32[]{:S(2)}) %all-to-all-start.1) | async-done | bytes 524320 | tf_op jit(solution)/shard_map/all_to_all | solution.py:45
  55.2 0.1 copy.31
  55.3 2.1 %fusion.11 = bf16[2,512,256]{2,1,0:T(8,128)(2,1)S(1)} fusion(bf16[1,512,2,512]{3,1,2,0:T(8,128)(2,1)S(1)} %get-tuple-element.26, bf16[1,512,2,512]{3,1,2,0:T(8,128)(2,1)S(1)} %get-tuple-element.25, bf16[1,256,2,256]{1,3,0,2:T(8,128)(2,1)} %get-tuple-element.28, bf16[1,256,2,256]{1,3,0,2:T(8,128)(2,1)S(1)} %get-tuple-element.27, ...), kind=kOutput, calls=%fused_computation.26 | convolution fusion | flops 807665664 | bytes 3670016 | tf_op jit(solution)/shard_map/dacq,cqr->dar/dot_general | solution.py:160
  57.4 1.9 %collective-permute-start = (bf16[2,256,256]{2,1,0:T(8,128)(2,1)S(1)}, bf16[2,256,256]{2,1,0:T(8,128)(2,1)S(1)}, u32[]{:S(2)}, u32[]{:S(2)}) collective-permute-start(bf16[2,256,256]{2,1,0:T(8,128)(2,1)S(1)} %get-tuple-element.24), channel_id=1, source_target_pairs={{0,1},{1,0},{2,3},{3,2},{4,5},{5,4},{6,7},{7,6},{8,9},{9,8},{10,11... | collective-permute-start | bytes 786440 | tf_op jit(solution)/shard_map/ppermute | solution.py:26
  59.3 0.8 select_reduce_fusion.4
  60.1 0.7 collective-permute-done
  60.8 0.5 convolution_bitcast_fusion.4
  61.3 2.5 %fusion.96 = (f32[1,512,256]{1,2,0:T(8,128)S(1)}, f32[1,512,256]{1,2,0:T(8,128)S(1)}) fusion(f32[2,2,512,256]{2,3,1,0:T(8,128)S(1)} %convolution_bitcast_fusion.4, f32[]{:T(128)S(6)} %convert_element_type.170, f32[512]{0:T(512)S(1)} %add_multiply_fusion, f32[256]{0:T(256)S(1)} %convert_multiply_fusion), kind=kLoop, calls=%fused_computation.128 | loop fusion | flops 2228224 | bytes 3148804 | tf_op jit(solution)/shard_map/add | solution.py:127
  63.8 0.1 fusion.19
  64.0 2.2 %collective-permute-start.1 = (bf16[2,256,256]{1,2,0:T(8,128)(2,1)S(1)}, bf16[2,256,256]{1,2,0:T(8,128)(2,1)S(1)}, u32[]{:S(2)}, u32[]{:S(2)}) collective-permute-start(bf16[2,256,256]{1,2,0:T(8,128)(2,1)S(1)} %get-tuple-element.22), channel_id=1, source_target_pairs={{0,2},{2,0},{1,3},{3,1},{4,6},{6,4},{5,7},{7,5},{8,10},{10,8},{9,1... | collective-permute-start | bytes 786440 | tf_op jit(solution)/shard_map/ppermute | solution.py:26
  66.2 0.8 select_reduce_fusion.3
  66.9 7.3 %collective-permute-done.1 = bf16[2,256,256]{1,2,0:T(8,128)(2,1)S(1)} collective-permute-done((bf16[2,256,256]{1,2,0:T(8,128)(2,1)S(1)}, bf16[2,256,256]{1,2,0:T(8,128)(2,1)S(1)}, u32[]{:S(2)}, u32[]{:S(2)}) %collective-permute-start.1) | collective-permute-done | bytes 262176 | tf_op jit(solution)/shard_map/ppermute | solution.py:26
  74.2 0.5 convolution_bitcast_fusion.3
  74.7 2.5 %fusion.84 = (f32[1,512,256]{1,2,0:T(8,128)S(1)}, f32[1,512,256]{1,2,0:T(8,128)S(1)}) fusion(f32[2,2,512,256]{2,3,1,0:T(8,128)S(1)} %convolution_bitcast_fusion.3, f32[]{:T(128)S(6)} %convert_element_type.173, f32[512]{0:T(512)S(1)} %add_multiply_fusion.1, f32[256]{0:T(256)S(1)} %convert_multiply_fusion), kind=kLoop, calls=%fused_computation.116 | loop fusion | flops 2228224 | bytes 3148804 | tf_op jit(solution)/shard_map/add | solution.py:127
  77.1 0.1 fusion.20
  77.3 6.2 %collective-permute-start.2 = (bf16[2,256,256]{1,2,0:T(8,128)(2,1)S(1)}, bf16[2,256,256]{1,2,0:T(8,128)(2,1)S(1)}, u32[]{:S(2)}, u32[]{:S(2)}) collective-permute-start(bf16[2,256,256]{1,2,0:T(8,128)(2,1)S(1)} %get-tuple-element.20), channel_id=1, source_target_pairs={{0,4},{4,0},{1,5},{5,1},{2,6},{6,2},{3,7},{7,3},{8,12},{12,8},{9,1... | collective-permute-start | bytes 786440 | tf_op jit(solution)/shard_map/ppermute | solution.py:26
  83.6 0.8 select_reduce_fusion.2
  84.3 5.0 %collective-permute-done.2 = bf16[2,256,256]{1,2,0:T(8,128)(2,1)S(1)} collective-permute-done((bf16[2,256,256]{1,2,0:T(8,128)(2,1)S(1)}, bf16[2,256,256]{1,2,0:T(8,128)(2,1)S(1)}, u32[]{:S(2)}, u32[]{:S(2)}) %collective-permute-start.2) | collective-permute-done | bytes 262176 | tf_op jit(solution)/shard_map/ppermute | solution.py:26
  89.3 0.5 convolution_bitcast_fusion.2
  89.7 2.5 %fusion.72 = (f32[1,512,256]{1,2,0:T(8,128)S(1)}, f32[1,512,256]{1,2,0:T(8,128)S(1)}) fusion(f32[2,2,512,256]{2,3,1,0:T(8,128)S(1)} %convolution_bitcast_fusion.2, f32[]{:T(128)S(6)} %convert_element_type.176, f32[512]{0:T(512)S(1)} %add_multiply_fusion.2, f32[256]{0:T(256)S(1)} %convert_multiply_fusion), kind=kLoop, calls=%fused_computation.104 | loop fusion | flops 2228224 | bytes 3148804 | tf_op jit(solution)/shard_map/add | solution.py:127
  92.2 0.1 fusion.21
  92.4 2.5 %collective-permute-start.3 = (bf16[2,256,256]{1,2,0:T(8,128)(2,1)S(1)}, bf16[2,256,256]{1,2,0:T(8,128)(2,1)S(1)}, u32[]{:S(2)}, u32[]{:S(2)}) collective-permute-start(bf16[2,256,256]{1,2,0:T(8,128)(2,1)S(1)} %get-tuple-element.18), channel_id=1, source_target_pairs={{0,32},{32,0},{64,96},{96,64},{128,160},{160,128},{192,224},{224,1... | collective-permute-start | bytes 786440 | tf_op jit(solution)/shard_map/ppermute | solution.py:26
  95.0 0.8 select_reduce_fusion.1
  95.7 5.5 %collective-permute-done.3 = bf16[2,256,256]{1,2,0:T(8,128)(2,1)S(1)} collective-permute-done((bf16[2,256,256]{1,2,0:T(8,128)(2,1)S(1)}, bf16[2,256,256]{1,2,0:T(8,128)(2,1)S(1)}, u32[]{:S(2)}, u32[]{:S(2)}) %collective-permute-start.3) | collective-permute-done | bytes 262176 | tf_op jit(solution)/shard_map/ppermute | solution.py:26
  101.2 0.5 convolution_bitcast_fusion.1
  101.7 2.5 %fusion.60 = (f32[1,512,256]{1,2,0:T(8,128)S(1)}, f32[1,512,256]{1,2,0:T(8,128)S(1)}) fusion(f32[2,2,512,256]{2,3,1,0:T(8,128)S(1)} %convolution_bitcast_fusion.1, f32[]{:T(128)S(6)} %convert_element_type.179, f32[512]{0:T(512)S(1)} %add_multiply_fusion.3, f32[256]{0:T(256)S(1)} %convert_multiply_fusion), kind=kLoop, calls=%fused_computation.92 | loop fusion | flops 2228224 | bytes 3148804 | tf_op jit(solution)/shard_map/add | solution.py:127
  104.1 0.1 fusion.22
  104.3 4.2 %collective-permute-start.4 = (bf16[2,256,256]{1,2,0:T(8,128)(2,1)S(1)}, bf16[2,256,256]{1,2,0:T(8,128)(2,1)S(1)}, u32[]{:S(2)}, u32[]{:S(2)}) collective-permute-start(bf16[2,256,256]{1,2,0:T(8,128)(2,1)S(1)} %get-tuple-element.16), channel_id=1, source_target_pairs={{0,64},{64,0},{32,96},{96,32},{128,192},{192,128},{160,224},{224,1... | collective-permute-start | bytes 786440 | tf_op jit(solution)/shard_map/ppermute | solution.py:26
  108.5 0.8 select_reduce_fusion
  109.3 4.8 %collective-permute-done.4 = bf16[2,256,256]{1,2,0:T(8,128)(2,1)S(1)} collective-permute-done((bf16[2,256,256]{1,2,0:T(8,128)(2,1)S(1)}, bf16[2,256,256]{1,2,0:T(8,128)(2,1)S(1)}, u32[]{:S(2)}, u32[]{:S(2)}) %collective-permute-start.4) | collective-permute-done | bytes 262176 | tf_op jit(solution)/shard_map/ppermute | solution.py:26
  114.1 0.5 convolution_bitcast_fusion
  114.6 2.5 %fusion.48 = (f32[1,512,256]{1,2,0:T(8,128)S(1)}, f32[1,512,256]{1,2,0:T(8,128)S(1)}) fusion(f32[2,2,512,256]{2,3,1,0:T(8,128)S(1)} %convolution_bitcast_fusion, f32[]{:T(128)S(6)} %convert_element_type.182, f32[256]{0:T(256)S(1)} %convert_multiply_fusion, f32[512]{0:T(512)S(1)} %add_multiply_fusion.4), kind=kLoop, calls=%fused_computation.80 | loop fusion | flops 2228224 | bytes 3148804 | tf_op jit(solution)/shard_map/add | solution.py:127
  117.0 0.1 fusion.23
  117.2 1.0 copy.35
  (24 shorter events, 0.4 us)
Async XLA Ops:
  1.5 22.0 %copy-start = (f32[5,2,4,512]{3,2,1,0:T(4,128)S(1)}, f32[5,2,4,512]{3,2,1,0:T(4,128)}, u32[]{:S(2)}) copy-start(f32[5,2,4,512]{3,2,1,0:T(4,128)} %param.6) | copy-start | bytes 245764
  1.5 22.0 %copy-start.1 = (s32[5,2,4,512]{3,2,1,0:T(4,128)S(1)}, s32[5,2,4,512]{3,2,1,0:T(4,128)}, u32[]{:S(2)}) copy-start(s32[5,2,4,512]{3,2,1,0:T(4,128)} %param.5) | copy-start | bytes 245764
  1.5 22.0 %copy-start.2 = (f32[5]{0:T(128)S(1)}, f32[5]{0:T(128)}, u32[]{:S(2)}) copy-start(f32[5]{0:T(128)} %param.7) | copy-start | bytes 64
  6.7 48.5 %all-to-all-start.1 = ((bf16[16,2,2,8,512]{4,3,1,2,0:T(8,128)(2,1)}), bf16[16,2,2,8,512]{4,3,1,2,0:T(8,128)(2,1)S(1)}, u32[]{:S(2)}, u32[]{:S(2)}) async-start(bf16[16,2,2,8,512]{4,3,1,2,0:T(8,128)(2,1)} %copy.30), calls=%async_computation.1 | async-start | bytes 1048576 | tf_op jit(solution)/shard_map/all_to_all | solution.py:45
  57.4 3.4 %collective-permute-start = (bf16[2,256,256]{2,1,0:T(8,128)(2,1)S(1)}, bf16[2,256,256]{2,1,0:T(8,128)(2,1)S(1)}, u32[]{:S(2)}, u32[]{:S(2)}) collective-permute-start(bf16[2,256,256]{2,1,0:T(8,128)(2,1)S(1)} %get-tuple-element.24), channel_id=1, source_target_pairs={{0,1},{1,0},{2,3},{3,2},{4,5},{5,4},{6,7},{7,6},{8,9},{9,8},{10,11... | collective-permute-start | bytes 786440 | tf_op jit(solution)/shard_map/ppermute | solution.py:26
  64.0 10.2 %collective-permute-start.1 = (bf16[2,256,256]{1,2,0:T(8,128)(2,1)S(1)}, bf16[2,256,256]{1,2,0:T(8,128)(2,1)S(1)}, u32[]{:S(2)}, u32[]{:S(2)}) collective-permute-start(bf16[2,256,256]{1,2,0:T(8,128)(2,1)S(1)} %get-tuple-element.22), channel_id=1, source_target_pairs={{0,2},{2,0},{1,3},{3,1},{4,6},{6,4},{5,7},{7,5},{8,10},{10,8},{9,1... | collective-permute-start | bytes 786440 | tf_op jit(solution)/shard_map/ppermute | solution.py:26
  77.3 11.9 %collective-permute-start.2 = (bf16[2,256,256]{1,2,0:T(8,128)(2,1)S(1)}, bf16[2,256,256]{1,2,0:T(8,128)(2,1)S(1)}, u32[]{:S(2)}, u32[]{:S(2)}) collective-permute-start(bf16[2,256,256]{1,2,0:T(8,128)(2,1)S(1)} %get-tuple-element.20), channel_id=1, source_target_pairs={{0,4},{4,0},{1,5},{5,1},{2,6},{6,2},{3,7},{7,3},{8,12},{12,8},{9,1... | collective-permute-start | bytes 786440 | tf_op jit(solution)/shard_map/ppermute | solution.py:26
  92.4 8.8 %collective-permute-start.3 = (bf16[2,256,256]{1,2,0:T(8,128)(2,1)S(1)}, bf16[2,256,256]{1,2,0:T(8,128)(2,1)S(1)}, u32[]{:S(2)}, u32[]{:S(2)}) collective-permute-start(bf16[2,256,256]{1,2,0:T(8,128)(2,1)S(1)} %get-tuple-element.18), channel_id=1, source_target_pairs={{0,32},{32,0},{64,96},{96,64},{128,160},{160,128},{192,224},{224,1... | collective-permute-start | bytes 786440 | tf_op jit(solution)/shard_map/ppermute | solution.py:26
  104.3 9.8 %collective-permute-start.4 = (bf16[2,256,256]{1,2,0:T(8,128)(2,1)S(1)}, bf16[2,256,256]{1,2,0:T(8,128)(2,1)S(1)}, u32[]{:S(2)}, u32[]{:S(2)}) collective-permute-start(bf16[2,256,256]{1,2,0:T(8,128)(2,1)S(1)} %get-tuple-element.16), channel_id=1, source_target_pairs={{0,64},{64,0},{32,96},{96,32},{128,192},{192,128},{160,224},{224,1... | collective-permute-start | bytes 786440 | tf_op jit(solution)/shard_map/ppermute | solution.py:26
where the time goes:
time: 119 us; the launch traced here: 118 us
  waiting for transfers between devices  39.6 us (33%)
  starting transfers between devices  33.8 us (28%)
  other arithmetic  28.1 us (24%)
  local copies, waits for them, and re-layouts  4.46 us (4%)
  matrix products  4.41 us (4%)
  blocking collectives  4.29 us (4%)
  between operations  3.59 us (3%)
    ppermute x5, waiting for transfers between devices, swapped(): return lax.ppermute(block, axis, route)  23.2 us
    ppermute x5, starting transfers between devices, swapped(): return lax.ppermute(block, axis, route)  17 us
    all_to_all x1, starting transfers between devices, moved_by_axis(): lax.all_to_all(parts, axes[k], split_axis=k, concat_axis=k, tiled=True)  16.8 us
    all_to_all x1, waiting for transfers between devices, moved_by_axis(): lax.all_to_all(parts, axes[k], split_axis=k, concat_axis=k, tiled=True)  16.3 us
    add x5, other arithmetic, merge_level(): own_re + partner_re  12.3 us
    another operation x4, other arithmetic  10.4 us
    all_to_all x1, blocking collectives, moved_by_axis(): lax.all_to_all(parts, axes[k], split_axis=k, concat_axis=k, tiled=True)  4.29 us
    reduce_sum x5, other arithmetic, interp_matrix(): jnp.sum(jnp.where(onehot, weight_rows[:, :, None], jnp.zeros((), weight_r...  3.77 us
  transfers between devices with their start and end apart: 6, of which 6 were waited for; matrix products, arithmetic and copies ran while one was open for 13% of the time, Pallas kernels for 0%

commit v1 on v0

v1 whole, which is shorter than its diff:
```python
import functools
import math

import jax
import jax.numpy as jnp
import numpy as np
from jax import lax
from jax.experimental import pallas as pl
from jax.experimental.pallas import tpu as pltpu
from jax.sharding import PartitionSpec as P

MESH = pl.DeviceIdType.MESH
NF = 256
ANGLES = 512
HALF = 256
LEVELS = 5
WIN = (24, 40, 72, 144, 256)
OUT = (40, 72, 144, 256, 512)
STACK = (4, 4, 2, 1, 1)
CHUNKS = 4


def chain(h, lesser, greater):
    low, starts = 0, [0] * LEVELS
    for level in range(LEVELS - 2, -1, -1):
        low = greater((h[level + 1] * HALF + low) // 2 - 1, 0)
        starts[level] = lesser(low, HALF - WIN[level])
    return starts


def beam_rows():
    rows = []
    for w in range(32):
        h = [w >> (4 - i) & 1 for i in range(5)]
        first = h[0] * HALF + chain(h, min, max)[0]
        rows.append(first + np.arange(WIN[0]))
    return np.concatenate(rows)


def tables():
    a = beam_rows()
    q = np.arange(512)
    beam = 2.0 * np.pi * (a[:, None] * q[None, :] % ANGLES) / ANGLES
    beam = np.concatenate([np.cos(beam), np.sin(beam)], axis=1)
    f = np.arange(NF)
    turn = 2.0 * np.pi * (f[:, None] * f[None, :] % NF) / NF
    cos = jnp.asarray(np.cos(turn), jnp.bfloat16)
    sin = jnp.asarray(np.sin(turn), jnp.bfloat16)
    real = jnp.concatenate([cos, -sin], axis=1)
    imag = jnp.concatenate([sin, cos], axis=1)
    both = jnp.stack([real.reshape(4, 8, 8, 512), imag.reshape(4, 8, 8, 512)], axis=2)
    both = both.transpose(1, 0, 2, 3, 4).reshape(8, 64, 512)
    return jnp.asarray(beam, jnp.bfloat16), both * jnp.bfloat16(1.0 / 16.0)


COS = np.polynomial.chebyshev.Chebyshev.interpolate(
    lambda s: np.cos(2 * np.pi * np.sqrt(s)), 7, domain=[0.0, 0.25]
).convert(kind=np.polynomial.Polynomial).coef
SIN = np.polynomial.chebyshev.Chebyshev.interpolate(
    lambda s: np.sinc(2 * np.sqrt(s)) * 2 * np.pi, 7, domain=[0.0, 0.25]
).convert(kind=np.polynomial.Polynomial).coef


def poly(coef, s):
    out = jnp.full_like(s, float(coef[-1]))
    for value in coef[-2::-1]:
        out = out * s + float(value)
    return out


def kernel(
    raw, taps, weights, shifts, beam_hbm, range_hbm, out,
    zbuf, beam, rtab, rexp, rawk, sbuf, rbuf, ph_c, ph_s, p0, p1, p2, p3, p4, x1, x2, x3, x4,
    zsend, zrecv, ssend, srecv, local,
):
    grp = lax.axis_index("grp")
    band = lax.axis_index("band")
    zh, x, c = band // 8, (band // 2) % 4, band % 2
    zl, y = grp // 4, grp % 4
    h = [c, x % 2, x // 2, y % 2, y // 2]
    mine = h[0] * 16 + h[1] * 8 + h[2] * 4 + h[3] * 2 + h[4]
    starts = chain(h, jnp.minimum, jnp.maximum)
    my_slot = (x * 2 + c) * 4 + y

    def zpeer(dz):
        return {"band": ((zh + dz) % 4) * 8 + x * 2 + c, "grp": grp}

    def near(o):
        xo, co, yo = (x + o // 2 % 4) % 4, (c + o % 2) % 2, (y + o // 8) % 4
        w = co * 16 + (xo % 2) * 8 + (xo // 2) * 4 + (yo % 2) * 2 + yo // 2
        return {"band": zh * 8 + xo * 2 + co, "grp": zl * 4 + yo}, w

    own = []
    own.append(pltpu.make_async_copy(beam_hbm, beam, local.at[0]))
    own.append(pltpu.make_async_copy(range_hbm, rtab, local.at[1]))
    for k in range(CHUNKS):
        own.append(
            pltpu.make_async_copy(
                raw.at[:, :, pl.ds(pl.multiple_of(zh * 4096 + k * 1024, 1024), 1024)],
                zbuf.at[k, zh],
                local.at[2 + k],
            )
        )
    for cp in own:
        cp.start()

    barrier = pltpu.get_barrier_semaphore()
    for dz in (2, 1, 3):
        pl.semaphore_signal(barrier, inc=1, device_id=zpeer(dz), device_id_type=MESH)

    def greet(o, carry):
        pl.semaphore_signal(barrier, inc=1, device_id=near(o)[0], device_id_type=MESH)
        return carry

    lax.fori_loop(1, 32, greet, 0)

    at = 0
    bases = []
    for level in range(LEVELS):
        rows, stack = OUT[level], STACK[level]
        if level < LEVELS - 1:
            first = h[level + 1] * HALF + starts[level + 1]
        else:
            first = 0
        j = (lax.broadcasted_iota(jnp.int32, (rows, 256), 0) + (h[level] * 512 + first)).astype(jnp.float32)
        r = lax.broadcasted_iota(jnp.int32, (rows, 256), 1).astype(jnp.float32)
        across = (j + 0.5) * (1.0 / 1024.0) - 0.5
        turns = (shifts[level] * across) * ((r + 256.0) * (1.0 / 256.0))
        turns = turns - jnp.round(turns)
        square = turns * turns
        cos = poly(COS, square) * math.sqrt(0.5)
        sin = poly(SIN, square) * turns * math.sqrt(0.5)
        for n in range(stack):
            ph_c[at + n * rows : at + (n + 1) * rows, :] = cos
            ph_s[at + n * rows : at + (n + 1) * rows, :] = sin
        bases.append(at)
        at += rows * stack

    pl.semaphore_wait(barrier, 34)

    zcopies = []
    for k in range(CHUNKS):
        for dz in (2, 1, 3):
            to = (zh + dz) % 4
            cp = pltpu.make_async_remote_copy(
                src_ref=raw.at[:, :, pl.ds(pl.multiple_of(to * 4096 + k * 1024, 1024), 1024)],
                dst_ref=zbuf.at[k, zh],
                send_sem=zsend.at[k, dz],
                recv_sem=zrecv.at[k, dz],
                device_id=zpeer(dz),
                device_id_type=MESH,
            )
            cp.start()
            zcopies.append(cp)

    for level, pm in enumerate((p0, p1, p2, p3, p4)):
        rows, stack, wide = OUT[level], STACK[level], WIN[level]
        mp = -(-rows * stack // 128) * 128
        kp = -(-wide * stack // 128) * 128
        tp = taps[level, h[level]]
        wt = weights[level, h[level]]
        if level < LEVELS - 1:
            first = h[level + 1] * HALF + starts[level + 1]
            lane = lax.broadcasted_iota(jnp.int32, (4, 512), 1)
            tp_all = jnp.full((4, 512), -1, jnp.int32)
            wt_all = jnp.zeros((4, 512), jnp.float32)
            for n in range(stack):
                turn = (512 + n * rows - first) % 512
                here = (lane >= n * rows) & (lane < (n + 1) * rows)
                tp_all = jnp.where(here, pltpu.roll(tp, turn, 1) + (n * wide - starts[level]), tp_all)
                wt_all = jnp.where(here, pltpu.roll(wt, turn, 1), wt_all)
            tp, wt = tp_all, wt_all
        ids = lax.broadcasted_iota(jnp.int32, (kp, mp), 0)
        total = jnp.zeros((kp, mp), jnp.float32)
        for s in range(4):
            total = total + jnp.where(tp[s : s + 1, :mp] == ids, wt[s : s + 1, :mp], 0.0)
        pm[...] = total.T[: rows * stack, : wide * stack].astype(jnp.bfloat16)

    own[1].wait()
    rexp[...] = jnp.zeros_like(rexp)
    for s in range(8):
        rexp[s * 128 : s * 128 + 64, 0:512] = rtab[s]
        rexp[s * 128 + 64 : s * 128 + 128, 512:1024] = rtab[s]

    def rotate(prod, level):
        base, rows = bases[level], OUT[level] * STACK[level]
        cos = ph_c[base : base + rows, :]
        sin = ph_s[base : base + rows, :]
        first, second = prod[:, 0:512], prod[:, 512:1024]
        add = first + second
        sub = first - second
        re = cos * add[:, :256] - sin * sub[:, 256:]
        im = cos * add[:, 256:] + sin * sub[:, :256]
        return re, im

    def dot(a, b):
        return jnp.dot(a, b, preferred_element_type=jnp.float32)

    def block_copy(k, o):
        dev, w = near(o)
        return pltpu.make_async_remote_copy(
            src_ref=sbuf.at[k, w],
            dst_ref=rbuf.at[k, my_slot],
            send_sem=ssend.at[k],
            recv_sem=srecv.at[k],
            device_id=dev,
            device_id_type=MESH,
        )

    def all_of(k):
        return pltpu.make_async_remote_copy(
            src_ref=sbuf.at[k, pl.ds(0, 31)],
            dst_ref=rbuf.at[k, pl.ds(0, 31)],
            send_sem=ssend.at[k],
            recv_sem=srecv.at[k],
            device_id=near(1)[0],
            device_id_type=MESH,
        )

    def send(k):
        own[2 + k].wait()
        for i in range(3):
            zcopies[k * 3 + i].wait_recv()
        for t in range(2):
            part = zbuf[k, :, :, :, t * 512 : (t + 1) * 512]
            real, imag = part[:, 0], part[:, 1]
            plain = jnp.stack([real, imag], axis=1).reshape(64, 512)
            turned = jnp.stack([imag, -real], axis=1).reshape(64, 512)
            rawk[t * 64 : (t + 1) * 64, 0:512] = plain
            rawk[t * 64 : (t + 1) * 64, 512:1024] = turned
        prod = lax.dot_general(
            beam[...], rawk[...], (((1,), (1,)), ((), ())), preferred_element_type=jnp.float32
        )
        prod = (prod * (1.0 / math.sqrt(512.0))).astype(jnp.bfloat16)
        sbuf[k] = prod.reshape(32, WIN[0], 128)

        def push(o, carry):
            block_copy(k, o).start()
            return carry

        lax.fori_loop(1, 32, push, 0)
        rbuf[k, my_slot] = sbuf[k, mine]

    def take(k):
        all_of(k).wait_recv()
        lhs = jnp.concatenate(
            [rbuf[k, s * 4 : s * 4 + 4].reshape(4 * WIN[0], 128) for s in range(8)], axis=1
        )
        sub0 = dot(lhs, rexp[...]).astype(jnp.bfloat16)
        re, im = rotate(dot(p0[...], sub0), 0)
        half = k % 2 * 512
        x1[k // 2, :, half : half + 256] = re.astype(jnp.bfloat16)
        x1[k // 2, :, half + 256 : half + 512] = im.astype(jnp.bfloat16)
        if k % 2 == 1:
            m = k // 2
            re, im = rotate(dot(p1[...], x1[m]), 1)
            for yh in range(2):
                x2[yh, :, m * 512 : m * 512 + 256] = re[yh * 144 : yh * 144 + 144].astype(jnp.bfloat16)
                x2[yh, :, m * 512 + 256 : m * 512 + 512] = im[yh * 144 : yh * 144 + 144].astype(jnp.bfloat16)

    own[0].wait()
    send(0)
    for k in range(1, CHUNKS):
        send(k)
        take(k - 1)
    take(CHUNKS - 1)
    for yh in range(2):
        re, im = rotate(dot(p2[...], x2[yh]), 2)
        for yb in range(2):
            x3[yh, :, yb * 512 : yb * 512 + 256] = re[yb * 144 : yb * 144 + 144].astype(jnp.bfloat16)
            x3[yh, :, yb * 512 + 256 : yb * 512 + 512] = im[yb * 144 : yb * 144 + 144].astype(jnp.bfloat16)
    for yh in range(2):
        re, im = rotate(dot(p3[...], x3[yh]), 3)
        x4[:, yh * 512 : yh * 512 + 256] = re.astype(jnp.bfloat16)
        x4[:, yh * 512 + 256 : yh * 512 + 512] = im.astype(jnp.bfloat16)
    re, im = rotate(dot(p4[...], x4[...]), 4)
    out[0] = re.astype(jnp.bfloat16)
    out[1] = im.astype(jnp.bfloat16)

    for cp in zcopies:
        cp.wait_send()
    for k in range(CHUNKS):
        all_of(k).wait_send()


def on_device(raw, taps, weights, shifts):
    beam, rtab = tables()
    rows = sum(o * s for o, s in zip(OUT, STACK))
    anyspace = pl.BlockSpec(memory_space=pl.ANY)
    vmem = pl.BlockSpec(memory_space=pltpu.VMEM)
    bf = jnp.bfloat16
    return pl.pallas_call(
        kernel,
        name="backproject",
        out_shape=jax.ShapeDtypeStruct((2, ANGLES, NF), bf),
        in_specs=[anyspace, vmem, vmem, pl.BlockSpec(memory_space=pltpu.SMEM), anyspace, anyspace],
        out_specs=vmem,
        scratch_shapes=[
            pltpu.VMEM((CHUNKS, 4, 2, 8, 1024), bf),
            pltpu.VMEM((768, 1024), bf),
            pltpu.VMEM((8, 64, 512), bf),
            pltpu.VMEM((1024, 1024), bf),
            pltpu.VMEM((128, 1024), bf),
            pltpu.VMEM((CHUNKS, 32, WIN[0], 128), bf),
            pltpu.VMEM((CHUNKS, 32, WIN[0], 128), bf),
            pltpu.VMEM((rows, 256), jnp.float32),
            pltpu.VMEM((rows, 256), jnp.float32),
        ]
        + [pltpu.VMEM((OUT[i] * STACK[i], WIN[i] * STACK[i]), bf) for i in range(LEVELS)]
        + [
            pltpu.VMEM((2, 160, 1024), bf),
            pltpu.VMEM((2, 144, 1024), bf),
            pltpu.VMEM((2, 144, 1024), bf),
            pltpu.VMEM((256, 1024), bf),
            pltpu.SemaphoreType.DMA((CHUNKS, 4)),
            pltpu.SemaphoreType.DMA((CHUNKS, 4)),
            pltpu.SemaphoreType.DMA((CHUNKS,)),
            pltpu.SemaphoreType.DMA((CHUNKS,)),
            pltpu.SemaphoreType.DMA((6,)),
        ],
        compiler_params=pltpu.CompilerParams(
            collective_id=0, has_side_effects=True, vmem_limit_bytes=56 << 20
        ),
    )(raw, taps, weights, shifts, beam, rtab)


def solution(mesh):
    return jax.shard_map(
        on_device,
        mesh=mesh,
        in_specs=(P(None, "band", "grp"), P(), P(), P()),
        out_specs=P(None, ("grp", "band"), None),
        check_vma=False,
    )
```

time: 119 us -> 59 us (0.50)
  the two profiles are of different devices: /device:TPU:40 before, /device:TPU:65 now
where the time goes in v1:
time: 59 us; the launch traced here: 58.8 us
  Pallas kernels  56.9 us (96%)
  local copies, waits for them, and re-layouts  1.87 us (3%)
    pallas_call x1, Pallas kernels, on_device(): pl.pallas_call(kernel, name='backproject', out_shape=jax.ShapeDtypeStruct...  56.9 us
    unnamed x1, local copies, waits for them, and re-layouts  1.87 us

profile of v1, /device:TPU:65, one launch (start us, length us, event | category | flops | bytes accessed | tf_op | source)
XLA Modules:
  0.0 58.8 jit_solution(15154684717338577140)
XLA Ops:
  0.0 56.9 %backproject.1 = bf16[2,512,256]{2,1,0:T(8,128)(2,1)} custom-call(bf16[2,8,16384]{2,1,0:T(8,128)(2,1)} %raw.1, s32[5,2,4,512]{3,2,1,0:T(4,128)} %taps.1, f32[5,2,4,512]{3,2,1,0:T(4,128)} %weights.1, f32[5]{0:T(128)} %shifts.1, bf16[768,1024]{1,0:T(8,128)(2,1)} %constant.10.clone.beam_hbm, bf16[8,64,512]{2,1,0:T(8,128)(2,1)} %constant.20.range_hbm), custom_call_target="tpu_custom_call" | custom-call | tf_op jit(solution)/shard_map/backproject/pallas_call | solution.py:292
  56.9 1.9 %copy.9 = bf16[2,512,256]{2,1,0:T(8,128)(2,1)} copy(bf16[2,512,256]{2,1,0:T(8,128)(2,1)} %backproject.1) | data formatting | bytes 1048576

commit v2 on v1

--- a/solution.py
+++ b/solution.py
@@ -69,9 +69,9 @@
 
 
 def kernel(
-    raw, taps, weights, shifts, beam_hbm, range_hbm, out,
-    zbuf, beam, rtab, rexp, rawk, sbuf, rbuf, ph_c, ph_s, p0, p1, p2, p3, p4, x1, x2, x3, x4,
-    zsend, zrecv, ssend, srecv, local,
+    raw, taps_hbm, weights_hbm, shifts_hbm, beam_hbm, range_hbm, out,
+    taps, weights, shifts, zbuf, beam, rtab, rexp, rawk, sbuf, rbuf, ph_c, ph_s, p0, p1, p2, p3, p4, x1, x2, x3, x4,
+    zsend, zrecv, ssend, srecv, local, zready, xyready,
 ):
     grp = lax.axis_index("grp")
     band = lax.axis_index("band")
@@ -86,7 +86,7 @@
         return {"band": ((zh + dz) % 4) * 8 + x * 2 + c, "grp": grp}
 
     def near(o):
-        xo, co, yo = (x + o // 2 % 4) % 4, (c + o % 2) % 2, (y + o // 8) % 4
+        xo, co, yo = (x + 2 + o // 2 % 4) % 4, (c + 1 + o % 2) % 2, (y + 2 + o // 8) % 4
         w = co * 16 + (xo % 2) * 8 + (xo // 2) * 4 + (yo % 2) * 2 + yo // 2
         return {"band": zh * 8 + xo * 2 + co, "grp": zl * 4 + yo}, w
 
@@ -101,18 +101,53 @@
                 local.at[2 + k],
             )
         )
-    for cp in own:
+    small = [
+        pltpu.make_async_copy(shifts_hbm, shifts, local.at[6]),
+        pltpu.make_async_copy(taps_hbm, taps, local.at[7]),
+        pltpu.make_async_copy(weights_hbm, weights, local.at[8]),
+    ]
+    barrier = pltpu.get_barrier_semaphore()
+    partner = {"band": zh * 8 + x * 2 + 1 - c, "grp": grp}
+    for dz in (2, 1, 3):
+        to = {"band": ((zh + dz) % 4) * 8 + x * 2, "grp": grp}
+        pl.semaphore_signal(barrier, inc=1, device_id=to, device_id_type=MESH)
+    pl.semaphore_signal(barrier, inc=1, device_id=partner, device_id_type=MESH)
+
+    def greet(o, carry):
+        to = {"band": zh * 8 + (x + o % 4) % 4 * 2 + 1, "grp": zl * 4 + (y + o // 4) % 4}
+        pl.semaphore_signal(barrier, inc=1, device_id=to, device_id_type=MESH)
+        return carry
+
+    lax.fori_loop(1, 16, greet, 0)
+
+    @pl.when(c == 0)
+    def _():
+        pl.semaphore_wait(barrier, 7)
+        pl.semaphore_signal(zready, inc=1, device_id=partner, device_id_type=MESH)
+
+    @pl.when(c == 1)
+    def _():
+        pl.semaphore_wait(zready, 1)
+
+    zcopies = []
+    for k in range(CHUNKS):
+        for dz in (2, 1, 3):
+            to = (zh + dz) % 4
+            cp = pltpu.make_async_remote_copy(
+                src_ref=raw.at[:, :, pl.ds(pl.multiple_of(to * 4096 + k * 1024, 1024), 1024)],
+                dst_ref=zbuf.at[k, zh],
+                send_sem=zsend.at[k, dz],
+                recv_sem=zrecv.at[k, dz],
+                device_id=zpeer(dz),
+                device_id_type=MESH,
+            )
+            cp.start()
+            zcopies.append(cp)
+
+    for cp in small + own:
         cp.start()
-
-    barrier = pltpu.get_barrier_semaphore()
-    for dz in (2, 1, 3):
-        pl.semaphore_signal(barrier, inc=1, device_id=zpeer(dz), device_id_type=MESH)
-
-    def greet(o, carry):
-        pl.semaphore_signal(barrier, inc=1, device_id=near(o)[0], device_id_type=MESH)
-        return carry
-
-    lax.fori_loop(1, 32, greet, 0)
+    for cp in small:
+        cp.wait()
 
     at = 0
     bases = []
@@ -135,23 +170,6 @@
             ph_s[at + n * rows : at + (n + 1) * rows, :] = sin
         bases.append(at)
         at += rows * stack
-
-    pl.semaphore_wait(barrier, 34)
-
-    zcopies = []
-    for k in range(CHUNKS):
-        for dz in (2, 1, 3):
-            to = (zh + dz) % 4
-            cp = pltpu.make_async_remote_copy(
-                src_ref=raw.at[:, :, pl.ds(pl.multiple_of(to * 4096 + k * 1024, 1024), 1024)],
-                dst_ref=zbuf.at[k, zh],
-                send_sem=zsend.at[k, dz],
-                recv_sem=zrecv.at[k, dz],
-                device_id=zpeer(dz),
-                device_id_type=MESH,
-            )
-            cp.start()
-            zcopies.append(cp)
 
     for level, pm in enumerate((p0, p1, p2, p3, p4)):
         rows, stack, wide = OUT[level], STACK[level], WIN[level]
@@ -213,7 +231,7 @@
             dst_ref=rbuf.at[k, pl.ds(0, 31)],
             send_sem=ssend.at[k],
             recv_sem=srecv.at[k],
-            device_id=near(1)[0],
+            device_id=near(0)[0],
             device_id_type=MESH,
         )
 
@@ -238,7 +256,8 @@
             block_copy(k, o).start()
             return carry
 
-        lax.fori_loop(1, 32, push, 0)
+        lax.fori_loop(0, 21, push, 0)
+        lax.fori_loop(22, 32, push, 0)
         rbuf[k, my_slot] = sbuf[k, mine]
 
     def take(k):
@@ -257,6 +276,15 @@
             for yh in range(2):
                 x2[yh, :, m * 512 : m * 512 + 256] = re[yh * 144 : yh * 144 + 144].astype(jnp.bfloat16)
                 x2[yh, :, m * 512 + 256 : m * 512 + 512] = im[yh * 144 : yh * 144 + 144].astype(jnp.bfloat16)
+
+    @pl.when(c == 0)
+    def _():
+        pl.semaphore_wait(xyready, 1)
+
+    @pl.when(c == 1)
+    def _():
+        pl.semaphore_wait(barrier, 31)
+        pl.semaphore_signal(xyready, inc=1, device_id=partner, device_id_type=MESH)
 
     own[0].wait()
     send(0)
@@ -286,16 +314,19 @@
 def on_device(raw, taps, weights, shifts):
     beam, rtab = tables()
     rows = sum(o * s for o, s in zip(OUT, STACK))
-    anyspace = pl.BlockSpec(memory_space=pl.ANY)
+    hbm = pl.BlockSpec(memory_space=pltpu.HBM)
     vmem = pl.BlockSpec(memory_space=pltpu.VMEM)
     bf = jnp.bfloat16
     return pl.pallas_call(
         kernel,
         name="backproject",
         out_shape=jax.ShapeDtypeStruct((2, ANGLES, NF), bf),
-        in_specs=[anyspace, vmem, vmem, pl.BlockSpec(memory_space=pltpu.SMEM), anyspace, anyspace],
+        in_specs=[hbm] * 6,
         out_specs=vmem,
         scratch_shapes=[
+            pltpu.VMEM((LEVELS, 2, 4, 512), jnp.int32),
+            pltpu.VMEM((LEVELS, 2, 4, 512), jnp.float32),
+            pltpu.SMEM((LEVELS,), jnp.float32),
             pltpu.VMEM((CHUNKS, 4, 2, 8, 1024), bf),
             pltpu.VMEM((768, 1024), bf),
             pltpu.VMEM((8, 64, 512), bf),
@@ -316,12 +347,14 @@
             pltpu.SemaphoreType.DMA((CHUNKS, 4)),
             pltpu.SemaphoreType.DMA((CHUNKS,)),
             pltpu.SemaphoreType.DMA((CHUNKS,)),
-            pltpu.SemaphoreType.DMA((6,)),
+            pltpu.SemaphoreType.DMA((9,)),
+            pltpu.SemaphoreType.REGULAR,
+            pltpu.SemaphoreType.REGULAR,
         ],
         compiler_params=pltpu.CompilerParams(
-            collective_id=0, has_side_effects=True, vmem_limit_bytes=56 << 20
+            collective_id=0, has_side_effects=True, vmem_limit_bytes=32 << 20
         ),
-    )(raw, taps, weights, shifts, beam, rtab)
+    )(*(pltpu.with_memory_space_constraint(a, pltpu.HBM) for a in (raw, taps, weights, shifts, beam, rtab)))
 
 
 def solution(mesh):

time: 59 us -> 54.7 us (0.927)
  the two profiles are of different devices: /device:TPU:65 before, /device:TPU:33 now
where the time goes in v2:
time: 54.7 us; the launch traced here: 54.6 us
  Pallas kernels  53.8 us (98%)
  local copies, waits for them, and re-layouts  0.8 us (1%)
    pallas_call x1, Pallas kernels, on_device(): pl.pallas_call(kernel, name='backproject', out_shape=jax.ShapeDtypeStruct...  53.8 us

profile of v2, /device:TPU:33, one launch (start us, length us, event | category | flops | bytes accessed | tf_op | source)
XLA Modules:
  0.0 54.6 jit_solution(6722704898713367689)
XLA Ops:
  0.0 53.8 %backproject.1 = bf16[2,512,256]{2,1,0:T(8,128)(2,1)S(1)} custom-call(bf16[2,8,16384]{2,1,0:T(8,128)(2,1)} %raw.1, s32[5,2,4,512]{3,2,1,0:T(4,128)} %taps_hbm.1, f32[5,2,4,512]{3,2,1,0:T(4,128)} %weights_hbm.1, f32[5]{0:T(128)} %shifts_hbm.1, bf16[768,1024]{1,0:T(8,128)(2,1)} %constant.10.clone.beam_hbm, bf16[8,64,512]{2,1,0:T(8,128)(2,1)} %constant.20.range_hbm), custom_call_target="tpu_custom_call" | custom-call | tf_op jit(solution)/shard_map/backproject/pallas_call | solution.py:320
  53.8 0.8 %copy.9 = bf16[2,512,256]{2,1,0:T(8,128)(2,1)} copy(bf16[2,512,256]{2,1,0:T(8,128)(2,1)S(1)} %backproject.1) | data formatting | bytes 1048576

commit v3 on v2

--- a/solution.py
+++ b/solution.py
@@ -49,7 +49,7 @@
     real = jnp.concatenate([cos, -sin], axis=1)
     imag = jnp.concatenate([sin, cos], axis=1)
     both = jnp.stack([real.reshape(4, 8, 8, 512), imag.reshape(4, 8, 8, 512)], axis=2)
-    both = both.transpose(1, 0, 2, 3, 4).reshape(8, 64, 512)
+    both = both.transpose(1, 0, 2, 3, 4).reshape(512, 512)
     return jnp.asarray(beam, jnp.bfloat16), both * jnp.bfloat16(1.0 / 16.0)
 
 
@@ -70,8 +70,8 @@
 
 def kernel(
     raw, taps_hbm, weights_hbm, shifts_hbm, beam_hbm, range_hbm, out,
-    taps, weights, shifts, zbuf, beam, rtab, rexp, rawk, sbuf, rbuf, ph_c, ph_s, p0, p1, p2, p3, p4, x1, x2, x3, x4,
-    zsend, zrecv, ssend, srecv, local, zready, xyready,
+    taps, weights, shifts, zbuf, beam, rtab, rawk, sbuf, rbuf, ph_c, ph_s, p0, p1, p2, p3, p4, x1, x2, x3, x4,
+    zsend, zrecv, ssend, srecv, local, known, xyready,
 ):
     grp = lax.axis_index("grp")
     band = lax.axis_index("band")
@@ -81,9 +81,6 @@
     mine = h[0] * 16 + h[1] * 8 + h[2] * 4 + h[3] * 2 + h[4]
     starts = chain(h, jnp.minimum, jnp.maximum)
     my_slot = (x * 2 + c) * 4 + y
-
-    def zpeer(dz):
-        return {"band": ((zh + dz) % 4) * 8 + x * 2 + c, "grp": grp}
 
     def near(o):
         xo, co, yo = (x + 2 + o // 2 % 4) % 4, (c + 1 + o % 2) % 2, (y + 2 + o // 8) % 4
@@ -106,46 +103,89 @@
         pltpu.make_async_copy(taps_hbm, taps, local.at[7]),
         pltpu.make_async_copy(weights_hbm, weights, local.at[8]),
     ]
+    for cp in small + own:
+        cp.start()
+
     barrier = pltpu.get_barrier_semaphore()
-    partner = {"band": zh * 8 + x * 2 + 1 - c, "grp": grp}
-    for dz in (2, 1, 3):
-        to = {"band": ((zh + dz) % 4) * 8 + x * 2, "grp": grp}
-        pl.semaphore_signal(barrier, inc=1, device_id=to, device_id_type=MESH)
-    pl.semaphore_signal(barrier, inc=1, device_id=partner, device_id_type=MESH)
+
+    def by_zh(values):
+        picked = values[0]
+        for i in range(1, 4):
+            picked = jnp.where(zh == i, values[i], picked)
+        return picked
+
+    def signal(sem, to):
+        pl.semaphore_signal(sem, inc=1, device_id=to, device_id_type=MESH)
+
+    def column(zo, co):
+        return {"band": zo * 8 + x * 2 + co, "grp": grp}
+
+    partner = column(zh, 1 - c)
+    soon = ((1, 0), (3, 0), (2, 0), (2, 1))
+    late = ((3, 1), (2, 3))
+    for pairs, core in ((soon, 0), (late, 1)):
+        for hears, speaks in pairs:
+
+            @pl.when(zh == speaks)
+            def _(hears=hears, core=core):
+                signal(barrier, column(hears, core))
+
+    signal(barrier, partner)
 
     def greet(o, carry):
-        to = {"band": zh * 8 + (x + o % 4) % 4 * 2 + 1, "grp": zl * 4 + (y + o // 4) % 4}
-        pl.semaphore_signal(barrier, inc=1, device_id=to, device_id_type=MESH)
+        signal(barrier, {"band": zh * 8 + (x + o % 4) % 4 * 2 + 1, "grp": zl * 4 + (y + o // 4) % 4})
         return carry
 
     lax.fori_loop(1, 16, greet, 0)
+
+    def tell(pairs):
+        for hears, speaks in pairs:
+
+            @pl.when(zh == hears)
+            def _(hears=hears, speaks=speaks):
+                pl.semaphore_signal(known.at[speaks], inc=1)
+                signal(known.at[speaks], partner)
+                for co in range(2):
+                    signal(known.at[hears], column(speaks, co))
 
     @pl.when(c == 0)
     def _():
-        pl.semaphore_wait(barrier, 7)
-        pl.semaphore_signal(zready, inc=1, device_id=partner, device_id_type=MESH)
-
-    @pl.when(c == 1)
-    def _():
-        pl.semaphore_wait(zready, 1)
-
-    zcopies = []
+        pl.semaphore_wait(barrier, by_zh((1, 3, 5, 3)))
+        tell(soon)
+
+    def hear_rest():
+        pl.semaphore_wait(barrier, by_zh((31, 31, 33, 33)))
+        tell(late)
+        signal(xyready, partner)
+
+    order = ((1, 3, 2), (0, 2, 3), (0, 1, 3), (0, 1, 2))
+
+    dests = [by_zh([o[p] for o in order]) for p in range(3)]
+
+    def meet(p):
+        pl.semaphore_wait(known.at[dests[p]], 1)
+
+    def zcopy(p, k):
+        return pltpu.make_async_remote_copy(
+            src_ref=raw.at[:, :, pl.ds(pl.multiple_of(dests[p] * 4096 + k * 1024, 1024), 1024)],
+            dst_ref=zbuf.at[k, zh],
+            send_sem=zsend.at[k, p],
+            recv_sem=zrecv.at[k, zh],
+            device_id=column(dests[p], c),
+            device_id_type=MESH,
+        )
+
+    def zsend_one(p, k):
+        zcopy(p, k).start()
+
+    meet(0)
     for k in range(CHUNKS):
-        for dz in (2, 1, 3):
-            to = (zh + dz) % 4
-            cp = pltpu.make_async_remote_copy(
-                src_ref=raw.at[:, :, pl.ds(pl.multiple_of(to * 4096 + k * 1024, 1024), 1024)],
-                dst_ref=zbuf.at[k, zh],
-                send_sem=zsend.at[k, dz],
-                recv_sem=zrecv.at[k, dz],
-                device_id=zpeer(dz),
-                device_id_type=MESH,
-            )
-            cp.start()
-            zcopies.append(cp)
-
-    for cp in small + own:
-        cp.start()
+        zsend_one(0, k)
+    pl.when((c == 1) & (zh != 2))(hear_rest)
+    meet(1)
+    for k in range(2):
+        zsend_one(1, k)
+    pl.when((c == 1) & (zh == 2))(hear_rest)
     for cp in small:
         cp.wait()
 
@@ -170,6 +210,18 @@
             ph_s[at + n * rows : at + (n + 1) * rows, :] = sin
         bases.append(at)
         at += rows * stack
+
+    meet(2)
+    for p, k in ((2, 0), (2, 1), (1, 2), (2, 2)):
+        zsend_one(p, k)
+    eager = (zl == 1) | (zl == 2)
+    rest = [(p, k) for k in range(3, CHUNKS) for p in (1, 2)]
+
+    @pl.when(eager)
+    def _():
+        for p, k in rest:
+            zcopy(p, k).start()
+
 
     for level, pm in enumerate((p0, p1, p2, p3, p4)):
         rows, stack, wide = OUT[level], STACK[level], WIN[level]
@@ -194,12 +246,6 @@
             total = total + jnp.where(tp[s : s + 1, :mp] == ids, wt[s : s + 1, :mp], 0.0)
         pm[...] = total.T[: rows * stack, : wide * stack].astype(jnp.bfloat16)
 
-    own[1].wait()
-    rexp[...] = jnp.zeros_like(rexp)
-    for s in range(8):
-        rexp[s * 128 : s * 128 + 64, 0:512] = rtab[s]
-        rexp[s * 128 + 64 : s * 128 + 128, 512:1024] = rtab[s]
-
     def rotate(prod, level):
         base, rows = bases[level], OUT[level] * STACK[level]
         cos = ph_c[base : base + rows, :]
@@ -237,8 +283,23 @@
 
     def send(k):
         own[2 + k].wait()
-        for i in range(3):
-            zcopies[k * 3 + i].wait_recv()
+        for i in range(1, 4):
+            came = (zh + i) % 4
+            pltpu.make_async_remote_copy(
+                src_ref=zbuf.at[k, came],
+                dst_ref=zbuf.at[k, came],
+                send_sem=zsend.at[k, 0],
+                recv_sem=zrecv.at[k, came],
+                device_id=column(came, c),
+                device_id_type=MESH,
+            ).wait_recv()
+        if k + 3 < CHUNKS:
+
+            @pl.when(jnp.logical_not(eager))
+            def _():
+                for p in (1, 2):
+                    zcopy(p, k + 3).start()
+
         for t in range(2):
             part = zbuf[k, :, :, :, t * 512 : (t + 1) * 512]
             real, imag = part[:, 0], part[:, 1]
@@ -262,10 +323,16 @@
 
     def take(k):
         all_of(k).wait_recv()
+        came = [rbuf[k, s * 4 : s * 4 + 4].reshape(4 * WIN[0], 128) for s in range(8)]
         lhs = jnp.concatenate(
-            [rbuf[k, s * 4 : s * 4 + 4].reshape(4 * WIN[0], 128) for s in range(8)], axis=1
-        )
-        sub0 = dot(lhs, rexp[...]).astype(jnp.bfloat16)
+            [
+                jnp.concatenate([piece[:, t * 64 : t * 64 + 64] for piece in came], axis=1)
+                for t in range(2)
+            ],
+            axis=0,
+        )
+        sub0 = dot(lhs, rtab[...]).astype(jnp.bfloat16)
+        sub0 = jnp.concatenate([sub0[: 4 * WIN[0]], sub0[4 * WIN[0] :]], axis=1)
         re, im = rotate(dot(p0[...], sub0), 0)
         half = k % 2 * 512
         x1[k // 2, :, half : half + 256] = re.astype(jnp.bfloat16)
@@ -281,12 +348,8 @@
     def _():
         pl.semaphore_wait(xyready, 1)
 
-    @pl.when(c == 1)
-    def _():
-        pl.semaphore_wait(barrier, 31)
-        pl.semaphore_signal(xyready, inc=1, device_id=partner, device_id_type=MESH)
-
     own[0].wait()
+    own[1].wait()
     send(0)
     for k in range(1, CHUNKS):
         send(k)
@@ -305,8 +368,9 @@
     out[0] = re.astype(jnp.bfloat16)
     out[1] = im.astype(jnp.bfloat16)
 
-    for cp in zcopies:
-        cp.wait_send()
+    for p in range(3):
+        for k in range(CHUNKS):
+            zcopy(p, k).wait_send()
     for k in range(CHUNKS):
         all_of(k).wait_send()
 
@@ -329,8 +393,7 @@
             pltpu.SMEM((LEVELS,), jnp.float32),
             pltpu.VMEM((CHUNKS, 4, 2, 8, 1024), bf),
             pltpu.VMEM((768, 1024), bf),
-            pltpu.VMEM((8, 64, 512), bf),
-            pltpu.VMEM((1024, 1024), bf),
+            pltpu.VMEM((512, 512), bf),
             pltpu.VMEM((128, 1024), bf),
             pltpu.VMEM((CHUNKS, 32, WIN[0], 128), bf),
             pltpu.VMEM((CHUNKS, 32, WIN[0], 128), bf),
@@ -348,7 +411,7 @@
             pltpu.SemaphoreType.DMA((CHUNKS,)),
             pltpu.SemaphoreType.DMA((CHUNKS,)),
             pltpu.SemaphoreType.DMA((9,)),
-            pltpu.SemaphoreType.REGULAR,
+            pltpu.SemaphoreType.REGULAR((4,)),
             pltpu.SemaphoreType.REGULAR,
         ],
         compiler_params=pltpu.CompilerParams(

time: 54.7 us -> 51.1 us (0.934)
  the two profiles are of different devices: /device:TPU:33 before, /device:TPU:449 now
where the time goes in v3:
time: 51.1 us; the launch traced here: 51 us
  Pallas kernels  50.2 us (98%)
  local copies, waits for them, and re-layouts  0.8 us (2%)
    pallas_call x1, Pallas kernels, on_device(): pl.pallas_call(kernel, name='backproject', out_shape=jax.ShapeDtypeStruct...  50.2 us

profile of v3, /device:TPU:449, one launch (start us, length us, event | category | flops | bytes accessed | tf_op | source)
XLA Modules:
  0.0 51.0 jit_solution(18395235117043768779)
XLA Ops:
  0.0 50.2 %backproject.1 = bf16[2,512,256]{2,1,0:T(8,128)(2,1)S(1)} custom-call(bf16[2,8,16384]{2,1,0:T(8,128)(2,1)} %raw.1, s32[5,2,4,512]{3,2,1,0:T(4,128)} %taps_hbm.1, f32[5,2,4,512]{3,2,1,0:T(4,128)} %weights_hbm.1, f32[5]{0:T(128)} %shifts_hbm.1, bf16[768,1024]{1,0:T(8,128)(2,1)} %constant.10.clone.beam_hbm, bf16[512,512]{1,0:T(8,128)(2,1)} %constant.20.range_hbm), custom_call_target="tpu_custom_call" | custom-call | tf_op jit(solution)/shard_map/backproject/pallas_call | solution.py:384
  50.2 0.8 %copy.9 = bf16[2,512,256]{2,1,0:T(8,128)(2,1)} copy(bf16[2,512,256]{2,1,0:T(8,128)(2,1)S(1)} %backproject.1) | data formatting | bytes 1048576

commit v4 on v3

--- a/solution.py
+++ b/solution.py
@@ -82,10 +82,17 @@
     starts = chain(h, jnp.minimum, jnp.maximum)
     my_slot = (x * 2 + c) * 4 + y
 
-    def near(o):
-        xo, co, yo = (x + 2 + o // 2 % 4) % 4, (c + 1 + o % 2) % 2, (y + 2 + o // 8) % 4
-        w = co * 16 + (xo % 2) * 8 + (xo // 2) * 4 + (yo % 2) * 2 + yo // 2
-        return {"band": zh * 8 + xo * 2 + co, "grp": zl * 4 + yo}, w
+    bands = [[zh * 8 + (x + dx) % 4 * 2 + (c + dc) % 2 for dc in range(2)] for dx in range(4)]
+    grps = [zl * 4 + (y + dy) % 4 for dy in range(4)]
+    w_c = [(c + dc) % 2 * 16 for dc in range(2)]
+    w_x = [(x + dx) % 2 * 8 + (x + dx) % 4 // 2 * 4 for dx in range(4)]
+    w_y = [(y + dy) % 2 * 2 + (y + dy) % 4 // 2 for dy in range(4)]
+    others = [(dx, dc, dy) for dx in range(4) for dc in range(2) for dy in range(4)][1:]
+    others.sort(key=lambda o: -min(o[0], 4 - o[0]) - min(o[2], 4 - o[2]))
+
+    def near(other):
+        dx, dc, dy = other
+        return {"band": bands[dx][dc], "grp": grps[dy]}, w_c[dc] + w_x[dx] + w_y[dy]
 
     own = []
     own.append(pltpu.make_async_copy(beam_hbm, beam, local.at[0]))
@@ -179,12 +186,13 @@
         zcopy(p, k).start()
 
     meet(0)
-    for k in range(CHUNKS):
-        zsend_one(0, k)
+    zsend_one(0, 0)
+    zsend_one(0, 1)
+    zsend_one(0, 2)
     pl.when((c == 1) & (zh != 2))(hear_rest)
     meet(1)
-    for k in range(2):
-        zsend_one(1, k)
+    zsend_one(1, 0)
+    zsend_one(1, 1)
     pl.when((c == 1) & (zh == 2))(hear_rest)
     for cp in small:
         cp.wait()
@@ -212,16 +220,8 @@
         at += rows * stack
 
     meet(2)
-    for p, k in ((2, 0), (2, 1), (1, 2), (2, 2)):
-        zsend_one(p, k)
-    eager = (zl == 1) | (zl == 2)
-    rest = [(p, k) for k in range(3, CHUNKS) for p in (1, 2)]
-
-    @pl.when(eager)
-    def _():
-        for p, k in rest:
-            zcopy(p, k).start()
-
+    zsend_one(2, 0)
+    zsend_one(2, 1)
 
     for level, pm in enumerate((p0, p1, p2, p3, p4)):
         rows, stack, wide = OUT[level], STACK[level], WIN[level]
@@ -246,6 +246,15 @@
             total = total + jnp.where(tp[s : s + 1, :mp] == ids, wt[s : s + 1, :mp], 0.0)
         pm[...] = total.T[: rows * stack, : wide * stack].astype(jnp.bfloat16)
 
+    pl.when(zl != 0)(lambda: pl.delay(2500))
+    zsend_one(1, 2)
+    zsend_one(2, 2)
+    pl.delay(2500)
+    pl.when(zl != 0)(lambda: pl.delay(2500))
+    zsend_one(0, 3)
+    zsend_one(1, 3)
+    zsend_one(2, 3)
+
     def rotate(prod, level):
         base, rows = bases[level], OUT[level] * STACK[level]
         cos = ph_c[base : base + rows, :]
@@ -277,7 +286,7 @@
             dst_ref=rbuf.at[k, pl.ds(0, 31)],
             send_sem=ssend.at[k],
             recv_sem=srecv.at[k],
-            device_id=near(0)[0],
+            device_id=near(others[0])[0],
             device_id_type=MESH,
         )
 
@@ -293,13 +302,6 @@
                 device_id=column(came, c),
                 device_id_type=MESH,
             ).wait_recv()
-        if k + 3 < CHUNKS:
-
-            @pl.when(jnp.logical_not(eager))
-            def _():
-                for p in (1, 2):
-                    zcopy(p, k + 3).start()
-
         for t in range(2):
             part = zbuf[k, :, :, :, t * 512 : (t + 1) * 512]
             real, imag = part[:, 0], part[:, 1]
@@ -313,12 +315,8 @@
         prod = (prod * (1.0 / math.sqrt(512.0))).astype(jnp.bfloat16)
         sbuf[k] = prod.reshape(32, WIN[0], 128)
 
-        def push(o, carry):
-            block_copy(k, o).start()
-            return carry
-
-        lax.fori_loop(0, 21, push, 0)
-        lax.fori_loop(22, 32, push, 0)
+        for other in others:
+            block_copy(k, other).start()
         rbuf[k, my_slot] = sbuf[k, mine]
 
     def take(k):

time: 51.1 us -> 48.5 us (0.949)
  Pallas kernels: 50.2 us -> 47.5 us
    pallas_call x1, Pallas kernels: 50.2 us -> 47.5 us  [on_device(): pl.pallas_call(kernel, name='backproject', out_shape=jax.ShapeDtypeStruct...]
where the time goes in v4:
time: 48.5 us; the launch traced here: 48.4 us
  Pallas kernels  47.5 us (98%)
  local copies, waits for them, and re-layouts  0.8 us (2%)
    pallas_call x1, Pallas kernels, on_device(): pl.pallas_call(kernel, name='backproject', out_shape=jax.ShapeDtypeStruct...  47.5 us

profile of v4, /device:TPU:449, one launch (start us, length us, event | category | flops | bytes accessed | tf_op | source)
XLA Modules:
  0.0 48.4 jit_solution(18158603859863943441)
XLA Ops:
  0.0 47.5 %backproject.1 = bf16[2,512,256]{2,1,0:T(8,128)(2,1)S(1)} custom-call(bf16[2,8,16384]{2,1,0:T(8,128)(2,1)} %raw.1, s32[5,2,4,512]{3,2,1,0:T(4,128)} %taps_hbm.1, f32[5,2,4,512]{3,2,1,0:T(4,128)} %weights_hbm.1, f32[5]{0:T(128)} %shifts_hbm.1, bf16[768,1024]{1,0:T(8,128)(2,1)} %constant.10.clone.beam_hbm, bf16[512,512]{1,0:T(8,128)(2,1)} %constant.20.range_hbm), custom_call_target="tpu_custom_call" | custom-call | tf_op jit(solution)/shard_map/backproject/pallas_call | solution.py:382
  47.6 0.8 %copy.9 = bf16[2,512,256]{2,1,0:T(8,128)(2,1)} copy(bf16[2,512,256]{2,1,0:T(8,128)(2,1)S(1)} %backproject.1) | data formatting | bytes 1048576

commit v5 on v4

--- a/solution.py
+++ b/solution.py
@@ -110,9 +110,6 @@
         pltpu.make_async_copy(taps_hbm, taps, local.at[7]),
         pltpu.make_async_copy(weights_hbm, weights, local.at[8]),
     ]
-    for cp in small + own:
-        cp.start()
-
     barrier = pltpu.get_barrier_semaphore()
 
     def by_zh(values):
@@ -144,6 +141,9 @@
         return carry
 
     lax.fori_loop(1, 16, greet, 0)
+
+    for cp in small + own:
+        cp.start()
 
     def tell(pairs):
         for hears, speaks in pairs:
@@ -246,11 +246,14 @@
             total = total + jnp.where(tp[s : s + 1, :mp] == ids, wt[s : s + 1, :mp], 0.0)
         pm[...] = total.T[: rows * stack, : wide * stack].astype(jnp.bfloat16)
 
-    pl.when(zl != 0)(lambda: pl.delay(2500))
+    pl.when((zl % 2 == 1) & (zh == 0))(lambda: pl.delay(1500))
+    pl.when((zl % 2 == 1) & (zh == 1))(lambda: pl.delay(500))
+    pl.when((zl % 2 == 1) & (zh == 2))(lambda: pl.delay(4000))
+    pl.when((zl % 2 == 1) & (zh == 3))(lambda: pl.delay(2500))
     zsend_one(1, 2)
     zsend_one(2, 2)
     pl.delay(2500)
-    pl.when(zl != 0)(lambda: pl.delay(2500))
+    pl.when(zl % 2 == 1)(lambda: pl.delay(2500))
     zsend_one(0, 3)
     zsend_one(1, 3)
     zsend_one(2, 3)

time: 48.5 us -> 48.1 us (level)
  the two profiles are of different devices: /device:TPU:449 before, /device:TPU:129 now
where the time goes in v5:
time: 48.1 us; the launch traced here: 48 us
  Pallas kernels  47.2 us (98%)
  local copies, waits for them, and re-layouts  0.8 us (2%)
    pallas_call x1, Pallas kernels, on_device(): pl.pallas_call(kernel, name='backproject', out_shape=jax.ShapeDtypeStruct...  47.2 us

profile of v5, /device:TPU:129, one launch (start us, length us, event | category | flops | bytes accessed | tf_op | source)
XLA Modules:
  0.0 48.0 jit_solution(3822965569814341933)
XLA Ops:
  0.0 47.2 %backproject.1 = bf16[2,512,256]{2,1,0:T(8,128)(2,1)S(1)} custom-call(bf16[2,8,16384]{2,1,0:T(8,128)(2,1)} %raw.1, s32[5,2,4,512]{3,2,1,0:T(4,128)} %taps_hbm.1, f32[5,2,4,512]{3,2,1,0:T(4,128)} %weights_hbm.1, f32[5]{0:T(128)} %shifts_hbm.1, bf16[768,1024]{1,0:T(8,128)(2,1)} %constant.10.clone.beam_hbm, bf16[512,512]{1,0:T(8,128)(2,1)} %constant.20.range_hbm), custom_call_target="tpu_custom_call" | custom-call | tf_op jit(solution)/shard_map/backproject/pallas_call | solution.py:385
  47.2 0.8 %copy.9 = bf16[2,512,256]{2,1,0:T(8,128)(2,1)} copy(bf16[2,512,256]{2,1,0:T(8,128)(2,1)S(1)} %backproject.1) | data formatting | bytes 1048576

commit v6 on v5

--- a/solution.py
+++ b/solution.py
@@ -82,17 +82,18 @@
     starts = chain(h, jnp.minimum, jnp.maximum)
     my_slot = (x * 2 + c) * 4 + y
 
-    bands = [[zh * 8 + (x + dx) % 4 * 2 + (c + dc) % 2 for dc in range(2)] for dx in range(4)]
+    bands = [[zh * 8 + (x + dx) % 4 * 2 + co for co in range(2)] for dx in range(4)]
     grps = [zl * 4 + (y + dy) % 4 for dy in range(4)]
-    w_c = [(c + dc) % 2 * 16 for dc in range(2)]
     w_x = [(x + dx) % 2 * 8 + (x + dx) % 4 // 2 * 4 for dx in range(4)]
     w_y = [(y + dy) % 2 * 2 + (y + dy) % 4 // 2 for dy in range(4)]
-    others = [(dx, dc, dy) for dx in range(4) for dc in range(2) for dy in range(4)][1:]
-    others.sort(key=lambda o: -min(o[0], 4 - o[0]) - min(o[2], 4 - o[2]))
+    places = sorted(
+        ((dx, dy) for dx in range(4) for dy in range(4)),
+        key=lambda o: -min(o[0], 4 - o[0]) - min(o[1], 4 - o[1]),
+    )
 
     def near(other):
-        dx, dc, dy = other
-        return {"band": bands[dx][dc], "grp": grps[dy]}, w_c[dc] + w_x[dx] + w_y[dy]
+        dx, co, dy = other
+        return {"band": bands[dx][co], "grp": grps[dy]}, co * 16 + w_x[dx] + w_y[dy]
 
     own = []
     own.append(pltpu.make_async_copy(beam_hbm, beam, local.at[0]))
@@ -289,7 +290,7 @@
             dst_ref=rbuf.at[k, pl.ds(0, 31)],
             send_sem=ssend.at[k],
             recv_sem=srecv.at[k],
-            device_id=near(others[0])[0],
+            device_id=near((1, 0, 0))[0],
             device_id_type=MESH,
         )
 
@@ -312,14 +313,20 @@
             turned = jnp.stack([imag, -real], axis=1).reshape(64, 512)
             rawk[t * 64 : (t + 1) * 64, 0:512] = plain
             rawk[t * 64 : (t + 1) * 64, 512:1024] = turned
-        prod = lax.dot_general(
-            beam[...], rawk[...], (((1,), (1,)), ((), ())), preferred_element_type=jnp.float32
-        )
-        prod = (prod * (1.0 / math.sqrt(512.0))).astype(jnp.bfloat16)
-        sbuf[k] = prod.reshape(32, WIN[0], 128)
-
-        for other in others:
-            block_copy(k, other).start()
+        for core in range(2):
+            prod = lax.dot_general(
+                beam[core * 384 : core * 384 + 384],
+                rawk[...],
+                (((1,), (1,)), ((), ())),
+                preferred_element_type=jnp.float32,
+            )
+            prod = (prod * (1.0 / math.sqrt(512.0))).astype(jnp.bfloat16)
+            sbuf[k, core * 16 : core * 16 + 16] = prod.reshape(16, WIN[0], 128)
+            for dx, dy in places:
+                if dx or dy:
+                    block_copy(k, (dx, core, dy)).start()
+                else:
+                    pl.when(c != core)(block_copy(k, (dx, core, dy)).start)
         rbuf[k, my_slot] = sbuf[k, mine]
 
     def take(k):

time: 48.1 us -> 47.9 us (level)
  the two profiles are of different devices: /device:TPU:129 before, /device:TPU:33 now
where the time goes in v6:
time: 47.9 us; the launch traced here: 47.8 us
  Pallas kernels  46.9 us (98%)
  local copies, waits for them, and re-layouts  0.8 us (2%)
    pallas_call x1, Pallas kernels, on_device(): pl.pallas_call(kernel, name='backproject', out_shape=jax.ShapeDtypeStruct...  46.9 us

profile of v6, /device:TPU:33, one launch (start us, length us, event | category | flops | bytes accessed | tf_op | source)
XLA Modules:
  0.0 47.8 jit_solution(2033016077613361530)
XLA Ops:
  0.0 46.9 %backproject.1 = bf16[2,512,256]{2,1,0:T(8,128)(2,1)S(1)} custom-call(bf16[2,8,16384]{2,1,0:T(8,128)(2,1)} %raw.1, s32[5,2,4,512]{3,2,1,0:T(4,128)} %taps_hbm.1, f32[5,2,4,512]{3,2,1,0:T(4,128)} %weights_hbm.1, f32[5]{0:T(128)} %shifts_hbm.1, bf16[768,1024]{1,0:T(8,128)(2,1)} %constant.10.clone.beam_hbm, bf16[512,512]{1,0:T(8,128)(2,1)} %constant.20.range_hbm), custom_call_target="tpu_custom_call" | custom-call | tf_op jit(solution)/shard_map/backproject/pallas_call | solution.py:392
  47.0 0.8 %copy.9 = bf16[2,512,256]{2,1,0:T(8,128)(2,1)} copy(bf16[2,512,256]{2,1,0:T(8,128)(2,1)S(1)} %backproject.1) | data formatting | bytes 1048576
